TPU v7x, 512 devices: a whole 4x4x16 slice. The times are simulated.
512 devices in a mesh: blk: 64 (over z, x), scale: 8 (over y, core).
Axes of the slice: x: 4, y: 4, z: 16, core: 2. Of those that a mesh axis runs over, the one named last changes fastest.
Arguments:
- start_block: float32 [64, 524288], P(None, ('blk', 'scale')), may hold values from -90 to 90
- blocks: bfloat16 [16384, 128, 128], P(('blk', 'scale')), may hold values from -0.1875 to 0.1875
- block_column: int32 [16384], P(('blk', 'scale')), may hold values from 0 to 7
- block_target: int32 [16384], P(('blk', 'scale')), may hold values from 0 to 15, as said below
- block_count: int32 [512], P(('blk', 'scale')), may hold values from 2 to 32, as said below
- partner: int32 [524288], P(('blk', 'scale')), may hold values from 0 to 1023, as said below
- degree: int32 [524288], P(('blk', 'scale')), may hold values from 1 to 16
Outputs:
- subspace: float32 [64, 524288], P(None, ('blk', 'scale'))
- rayleigh: float32 [64, 64], replicated
Inputs may be any that keep to these rules, and one draw needn't show every extreme that they name: block_count[g] is the number of live slots of row group g; it is at least 2; some row group has all 32 slots live in every draw. In each row group, slots c < 2 have block_target of 8 or more, and all other slots have block_target below 8. Within each row group, partner is a permutation of 0 to 1023, and the pairing is mutual: if node i of group (b, s) has partner j, then node j of group (b, s xor 1) has partner i.
All inputs are finite; a program needn't handle non-finite values.
Results may differ from a plain program's by a relative error of at most 0.0011.
Values may be sent and summed in bfloat16 or wider, within the bound.
No kernel may reach another device: no remote copies, remote signals or barrier semaphores. Data moves between devices by JAX's collectives and lax.ppermute only.
A program may use at most 64 MiB of HBM per device.

v0:
```python
import jax
import jax.numpy as jnp
from jax import lax
from jax.sharding import PartitionSpec as P

ITERS = 2
FULL_PRECISION = lax.Precision.HIGHEST


def from_behind(block, axis, distance):
    devices = range(lax.axis_size(axis))
    route = [((i - distance) % len(devices), i) for i in devices]
    return lax.ppermute(block, axis, route)


def swapped(array, axis, apart):
    return lax.ppermute(array, axis, [(i, i ^ 1 << apart) for i in range(lax.axis_size(axis))])


def pick_rows(onehot, source):
    picked = jnp.einsum(
        "cr,krj->ckj", onehot.astype(jnp.bfloat16), source, preferred_element_type=jnp.float32
    )
    return picked.astype(jnp.bfloat16)


def place_rows(onehot, partial_terms):
    return jnp.einsum("cr,ckj->krj", onehot, partial_terms, precision=FULL_PRECISION)


def slot_masks(columns, targets, slot_count, row_blocks):
    live_mask = (jnp.arange(columns.shape[0]) < slot_count[0]).astype(jnp.float32)[:, None]
    onecol = (columns[:, None] == jnp.arange(row_blocks)[None, :]).astype(jnp.float32) * live_mask
    onetgt = (targets[:, None] == jnp.arange(2 * row_blocks)[None, :]).astype(
        jnp.float32
    ) * live_mask
    return (onecol, onetgt)


def forward_terms(source, weights, onecol):
    picked = pick_rows(onecol, source)
    return jnp.einsum("cki,cji->ckj", picked, weights, preferred_element_type=jnp.float32)


def backward_terms(stacked, weights, onetgt):
    picked = pick_rows(onetgt, stacked)
    return jnp.einsum("ckj,cji->cki", picked, weights, preferred_element_type=jnp.float32)


def over_slots(term_fn, slot_total, initial):
    return jax.tree.map(jnp.add, initial, term_fn(0, slot_total))


def apply_operator(
    vectors, inv_sqrt_degree, blocks, block_column, block_target, block_count, partner
):
    vector_count, node_rows = vectors.shape
    row_blocks = node_rows // 128
    scaled = (vectors * inv_sqrt_degree[None, :]).astype(jnp.bfloat16)
    own_vectors = scaled.reshape(vector_count, row_blocks, 128)
    next_vectors = from_behind(own_vectors, "blk", -1)
    stacked = jnp.concatenate([own_vectors, next_vectors], axis=1)
    onecol, onetgt = slot_masks(block_column, block_target, block_count, row_blocks)
    empty_sum = jnp.zeros((vector_count, row_blocks, 128), jnp.float32)

    def local_terms(first_slot, slot_width):
        forward = forward_terms(own_vectors, blocks, onecol)
        backward = backward_terms(stacked, blocks, onetgt)
        nearby = place_rows(onetgt[:, :row_blocks], forward) + place_rows(onecol, backward)
        return (nearby, place_rows(onetgt[:, row_blocks:], forward))

    nearby, ahead_sum = over_slots(local_terms, blocks.shape[0], (empty_sum, empty_sum))
    surface = nearby + from_behind(ahead_sum.astype(jnp.bfloat16), "blk", 1).astype(ahead_sum.dtype)
    partner_vectors = swapped(scaled, "scale", 0)
    crossed = jnp.take(partner_vectors, partner, axis=1).astype(jnp.float32)
    return vectors + inv_sqrt_degree[None, :] * (surface.reshape(vector_count, node_rows) + crossed)


def shards(start_block, blocks, block_column, block_target, block_count, partner, degree):
    inv_sqrt_degree = 1.0 / jnp.sqrt(degree.astype(jnp.float32))
    vector_count = start_block.shape[0]
    node_total = start_block.shape[1] * lax.axis_size("blk") * lax.axis_size("scale")

    def operate(vectors):
        return apply_operator(
            vectors, inv_sqrt_degree, blocks, block_column, block_target, block_count, partner
        )

    subspace = start_block
    for sweep_index in range(ITERS):
        orthonormal_images = operate(subspace)
        local_gram = jnp.dot(orthonormal_images, orthonormal_images.T, precision=FULL_PRECISION)
        gram_matrix = lax.psum(local_gram, ("blk", "scale")) / node_total
        factor = jnp.linalg.cholesky(gram_matrix)
        factor_inverse = jax.scipy.linalg.solve_triangular(
            factor, jnp.eye(vector_count, dtype=jnp.float32), lower=True
        )
        subspace = jnp.dot(factor_inverse, orthonormal_images, precision=FULL_PRECISION)
    images = operate(subspace)
    local_projection = jnp.dot(subspace, images.T, precision=FULL_PRECISION)
    rayleigh = lax.psum(local_projection, ("blk", "scale")) / node_total
    return (subspace, rayleigh)


def solution(mesh):
    return jax.shard_map(
        shards,
        mesh=mesh,
        in_specs=(
            P(None, ("blk", "scale")),
            P(("blk", "scale"), None, None),
            P(("blk", "scale")),
            P(("blk", "scale")),
            P(("blk", "scale")),
            P(("blk", "scale")),
            P(("blk", "scale")),
        ),
        out_specs=(P(None, ("blk", "scale")), P()),
        check_vma=False,
    )
```

profile of v0, /device:TPU:1, one launch (start us, length us, event | category | flops | bytes accessed | tf_op | source)
XLA Modules:
  0.0 408.4 jit_solution(9733213956229735695)
XLA Ops:
  0.6 0.8 convert_rsqrt_fusion
  1.4 1.0 fusion.136
  2.4 14.1 %collective-permute-start = (bf16[64,8,128]{2,1,0:T(8,128)(2,1)S(1)}, bf16[64,8,128]{2,1,0:T(8,128)(2,1)S(1)}, u32[]{:S(2)}, u32[]{:S(2)}) collective-permute-start(bf16[64,8,128]{2,1,0:T(8,128)(2,1)S(1)} %bitcast.141), channel_id=1, source_target_pairs={{8,0},{16,8},{24,16},{32,24},{40,32},{48,40},{56,48},{64,56},{72,6... | collective-permute-start | bytes 393224 | tf_op jit(solution)/shard_map/ppermute | solution.py:13
  17.2 0.6 copy-done.10
  18.6 0.8 fusion.18
  19.4 1.2 fusion.3
  20.6 1.9 collective-permute-start.1
  22.6 2.9 collective-permute-start.2
  25.5 1.2 fusion.16
  26.8 0.6 compare_and_fusion
  28.2 3.2 gather_fusion
  31.6 1.9 convert_add_fusion.2
  33.5 0.7 copy-done.7
  34.2 0.4 fusion.118
  34.6 103.9 %psum.21 = f32[64,64]{0,1:T(8,128)S(1)} all-reduce(f32[64,64]{0,1:T(8,128)S(1)} %fusion.118), channel_id=1, replica_groups=mesh['blk'=64,'scale'=8] {'blk','scale'}, use_global_device_ids=true, to_apply=%region_0.0 | all-reduce | flops 4096 | bytes 32768 | tf_op jit(solution)/shard_map/psum | solution.py:93
  138.7 5.8 %cholesky.44 = f32[64,64]{1,0:T(8,128)S(1)} custom-call(f32[64,64]{1,0:T(8,128)S(1)} %fusion.60), custom_call_target="Cholesky" | custom-call | tf_op jit(solution)/shard_map/jit(cholesky)/cholesky | solution.py:94
  144.6 0.6 compare_reduce_fusion.1
  145.2 0.7 fusion.55
  145.9 4.9 %custom-call.6 = f32[1,64,64]{1,2,0:T(8,128)S(1)} custom-call(f32[1,64,64]{2,1,0:T(8,128)S(1)} %fusion.55), custom_call_target="InvertDiagBlocksLowerTriangular" | custom-call | tf_op jit(solution)/shard_map/jit(_solve_triangular)/triangular_solve | solution.py:95
  151.5 0.6 copy-done.4
  152.5 1.9 collective-permute-start.3
  154.4 2.9 collective-permute-start.5
  157.3 0.8 fusion.20
  158.1 1.2 fusion.4
  159.4 3.8 collective-permute-start.4
  163.2 1.2 fusion.13
  165.4 3.2 gather_fusion.1
  168.7 0.9 collective-permute-done.4
  169.6 1.9 convert_add_fusion.1
  171.6 0.7 copy-done.8
  172.7 99.6 %psum.22 = f32[64,64]{0,1:T(8,128)S(1)} all-reduce(f32[64,64]{0,1:T(8,128)S(1)} %fusion.122), channel_id=1, replica_groups=mesh['blk'=64,'scale'=8] {'blk','scale'}, use_global_device_ids=true, to_apply=%region_3.7 | all-reduce | flops 4096 | bytes 32768 | tf_op jit(solution)/shard_map/psum | solution.py:93
  272.4 5.8 %cholesky.55 = f32[64,64]{1,0:T(8,128)S(1)} custom-call(f32[64,64]{1,0:T(8,128)S(1)} %fusion.58), custom_call_target="Cholesky" | custom-call | tf_op jit(solution)/shard_map/jit(cholesky)/cholesky | solution.py:94
  278.3 0.6 compare_reduce_fusion
  278.9 0.7 fusion.56
  279.6 4.9 %custom-call.7 = f32[1,64,64]{1,2,0:T(8,128)S(1)} custom-call(f32[1,64,64]{2,1,0:T(8,128)S(1)} %fusion.56), custom_call_target="InvertDiagBlocksLowerTriangular" | custom-call | tf_op jit(solution)/shard_map/jit(_solve_triangular)/triangular_solve | solution.py:95
  285.2 0.7 copy-done.5
  286.2 4.8 %collective-permute-start.6 = (bf16[64,8,128]{2,1,0:T(8,128)(2,1)S(1)}, bf16[64,8,128]{2,1,0:T(8,128)(2,1)S(1)}, u32[]{:S(2)}, u32[]{:S(2)}) collective-permute-start(bf16[64,8,128]{2,1,0:T(8,128)(2,1)S(1)} %bitcast.145), channel_id=1, source_target_pairs={{8,0},{16,8},{24,16},{32,24},{40,32},{48,40},{56,48},{64,56},{72,6... | collective-permute-start | bytes 393224 | tf_op jit(solution)/shard_map/ppermute | solution.py:13
  291.0 2.9 collective-permute-start.8
  293.9 0.8 fusion.22
  294.7 1.3 fusion.5
  296.0 2.1 collective-permute-start.7
  298.1 1.2 fusion.10
  300.3 3.2 gather_fusion.2
  303.7 2.6 collective-permute-done.7
  306.3 1.2 convert_add_fusion
  307.5 0.7 copy-done.9
  308.6 99.2 %psum.23 = f32[64,64]{0,1:T(8,128)S(1)} all-reduce(f32[64,64]{0,1:T(8,128)S(1)} %fusion.24), channel_id=1, replica_groups=mesh['blk'=64,'scale'=8] {'blk','scale'}, use_global_device_ids=true, to_apply=%region_4.8 | all-reduce | flops 4096 | bytes 32768 | tf_op jit(solution)/shard_map/psum | solution.py:101
  407.7 0.7 copy.26
  (74 shorter events, 7.0 us)
Async XLA Ops:
  0.6 17.9 %copy-start = (bf16[32,128,128]{2,1,0:T(8,128)(2,1)S(1)}, bf16[32,128,128]{2,1,0:T(8,128)(2,1)}, u32[]{:S(2)}) copy-start(bf16[32,128,128]{2,1,0:T(8,128)(2,1)} %param.13) | copy-start | bytes 3145732
  2.4 24.9 %collective-permute-start = (bf16[64,8,128]{2,1,0:T(8,128)(2,1)S(1)}, bf16[64,8,128]{2,1,0:T(8,128)(2,1)S(1)}, u32[]{:S(2)}, u32[]{:S(2)}) collective-permute-start(bf16[64,8,128]{2,1,0:T(8,128)(2,1)S(1)} %bitcast.141), channel_id=1, source_target_pairs={{8,0},{16,8},{24,16},{32,24},{40,32},{48,40},{56,48},{64,56},{72,6... | collective-permute-start | bytes 393224 | tf_op jit(solution)/shard_map/ppermute | solution.py:13
  17.2 0.7 copy-start.10
  17.9 9.5 %copy-start.3 = (f32[32]{0:T(128)}, f32[32]{0:T(128)S(1)}, u32[]{:S(2)}) copy-start(f32[32]{0:T(128)S(1)} %compare_convert_fusion) | copy-start | bytes 388
  17.9 0.7 copy-start.15
  19.4 3.2 copy-start.1
  20.6 11.0 %collective-permute-start.1 = (bf16[64,8,128]{2,1,0:T(8,128)(2,1)S(1)}, bf16[64,8,128]{2,1,0:T(8,128)(2,1)S(1)}, u32[]{:S(2)}, u32[]{:S(2)}) collective-permute-start(bf16[64,8,128]{2,1,0:T(8,128)(2,1)S(1)} %fusion.3), channel_id=1, source_target_pairs={{504,0},{0,8},{8,16},{16,24},{24,32},{32,40},{40,48},{48,56},{56,6... | collective-permute-start | bytes 393224 | tf_op jit(solution)/shard_map/ppermute | solution.py:13
  22.6 4.1 %copy-start.14 = (s32[1024]{0:T(1024)S(1)}, s32[1024]{0:T(1024)}, u32[]{:S(2)}) copy-start(s32[1024]{0:T(1024)} %param.17) | copy-start | bytes 12292
  22.6 5.4 %collective-permute-start.2 = (bf16[64,1024]{1,0:T(8,128)(2,1)S(1)}, bf16[64,1024]{1,0:T(8,128)(2,1)S(1)}, u32[]{:S(2)}, u32[]{:S(2)}) collective-permute-start(bf16[64,1024]{1,0:T(8,128)(2,1)S(1)} %multiply_convert_fusion.2), channel_id=1, source_target_pairs={{0,1},{1,0},{2,3},{3,2},{4,5},{5,4},{6,7},{7,6},{8,9},{9,8},{10,11... | collective-permute-start | bytes 393224 | tf_op jit(solution)/shard_map/ppermute | solution.py:17
  33.5 0.7 copy-start.7
  151.5 0.7 copy-start.4
  151.5 0.7 copy-start.11
  152.5 12.0 %collective-permute-start.3 = (bf16[64,8,128]{2,1,0:T(8,128)(2,1)S(1)}, bf16[64,8,128]{2,1,0:T(8,128)(2,1)S(1)}, u32[]{:S(2)}, u32[]{:S(2)}) collective-permute-start(bf16[64,8,128]{2,1,0:T(8,128)(2,1)S(1)} %bitcast.148), channel_id=1, source_target_pairs={{8,0},{16,8},{24,16},{32,24},{40,32},{48,40},{56,48},{64,56},{72,6... | collective-permute-start | bytes 393224 | tf_op jit(solution)/shard_map/ppermute | solution.py:13
  154.4 10.8 %collective-permute-start.5 = (bf16[64,1024]{1,0:T(8,128)(2,1)S(1)}, bf16[64,1024]{1,0:T(8,128)(2,1)S(1)}, u32[]{:S(2)}, u32[]{:S(2)}) collective-permute-start(bf16[64,1024]{1,0:T(8,128)(2,1)S(1)} %get-tuple-element.7), channel_id=1, source_target_pairs={{0,1},{1,0},{2,3},{3,2},{4,5},{5,4},{6,7},{7,6},{8,9},{9,8},{10,11... | collective-permute-start | bytes 393224 | tf_op jit(solution)/shard_map/ppermute | solution.py:17
  159.4 5.1 %copy-start.16 = (s32[32]{0:T(128)S(1)}, s32[32]{0:T(128)}, u32[]{:S(2)}) copy-start(s32[32]{0:T(128)} %param.15) | copy-start | bytes 388
  159.4 10.3 %collective-permute-start.4 = (bf16[64,8,128]{2,1,0:T(8,128)(2,1)S(1)}, bf16[64,8,128]{2,1,0:T(8,128)(2,1)S(1)}, u32[]{:S(2)}, u32[]{:S(2)}) collective-permute-start(bf16[64,8,128]{2,1,0:T(8,128)(2,1)S(1)} %fusion.4), channel_id=1, source_target_pairs={{504,0},{0,8},{8,16},{16,24},{24,32},{32,40},{40,48},{48,56},{56,6... | collective-permute-start | bytes 393224 | tf_op jit(solution)/shard_map/ppermute | solution.py:13
  171.5 0.7 copy-start.8
  285.1 22.4 %copy-start.2 = (f32[64,1024]{1,0:T(8,128)}, f32[64,1024]{1,0:T(8,128)S(1)}, u32[]{:S(2)}) copy-start(f32[64,1024]{1,0:T(8,128)S(1)} %get-tuple-element.10) | copy-start | bytes 786436
  285.2 0.7 copy-start.5
  285.2 0.7 copy-start.12
  286.2 13.2 %collective-permute-start.6 = (bf16[64,8,128]{2,1,0:T(8,128)(2,1)S(1)}, bf16[64,8,128]{2,1,0:T(8,128)(2,1)S(1)}, u32[]{:S(2)}, u32[]{:S(2)}) collective-permute-start(bf16[64,8,128]{2,1,0:T(8,128)(2,1)S(1)} %bitcast.145), channel_id=1, source_target_pairs={{8,0},{16,8},{24,16},{32,24},{40,32},{48,40},{56,48},{64,56},{72,6... | collective-permute-start | bytes 393224 | tf_op jit(solution)/shard_map/ppermute | solution.py:13
  291.0 9.1 %collective-permute-start.8 = (bf16[64,1024]{1,0:T(8,128)(2,1)S(1)}, bf16[64,1024]{1,0:T(8,128)(2,1)S(1)}, u32[]{:S(2)}, u32[]{:S(2)}) collective-permute-start(bf16[64,1024]{1,0:T(8,128)(2,1)S(1)} %get-tuple-element.9), channel_id=1, source_target_pairs={{0,1},{1,0},{2,3},{3,2},{4,5},{5,4},{6,7},{7,6},{8,9},{9,8},{10,11... | collective-permute-start | bytes 393224 | tf_op jit(solution)/shard_map/ppermute | solution.py:17
  296.0 3.4 copy-start.17
  296.0 10.3 %collective-permute-start.7 = (bf16[64,8,128]{2,1,0:T(8,128)(2,1)S(1)}, bf16[64,8,128]{2,1,0:T(8,128)(2,1)S(1)}, u32[]{:S(2)}, u32[]{:S(2)}) collective-permute-start(bf16[64,8,128]{2,1,0:T(8,128)(2,1)S(1)} %fusion.5), channel_id=1, source_target_pairs={{504,0},{0,8},{8,16},{16,24},{24,32},{32,40},{40,48},{48,56},{56,6... | collective-permute-start | bytes 393224 | tf_op jit(solution)/shard_map/ppermute | solution.py:13
  303.5 2.7 copy-start.6
  303.5 2.7 copy-start.13
  307.5 0.7 copy-start.9
where the time goes:
time: 409 us; the launch traced here: 408 us
  blocking collectives  303 us (74%)
  starting transfers between devices  37.3 us (9%)
  other arithmetic  26.5 us (6%)
  matrix products  20.7 us (5%)
  local copies, waits for them, and re-layouts  15.8 us (4%)
    psum x2, blocking collectives, shards(): gram_matrix = lax.psum(local_gram, ('blk', 'scale')) / node_total  204 us
    psum x1, blocking collectives, shards(): rayleigh = lax.psum(local_projection, ('blk', 'scale')) / node_total  99.2 us
    ppermute x6, starting transfers between devices, from_behind(): return lax.ppermute(block, axis, route)  28.7 us
    another operation x6, other arithmetic, shards(): factor = jnp.linalg.cholesky(gram_matrix)  13 us
    dot_general x9, matrix products, place_rows(): jnp.einsum('cr,ckj->krj', onehot, partial_terms, precision=FULL_PRECISION)  12.5 us
    another operation x4, other arithmetic, shards(): jax.scipy.linalg.solve_triangular(factor, jnp.eye(vector_count, dtype=jnp...  11.1 us
    gather x6, local copies, waits for them, and re-layouts, apply_operator(): crossed = jnp.take(partner_vectors, partner, axis=1).astype(jnp.float32)  10 us
    ppermute x3, starting transfers between devices, swapped(): lax.ppermute(array, axis, [(i, i ^ 1 << apart) for i in range(lax.axis_si...  8.6 us
  transfers between devices with their start and end apart: 9, of which 2 were waited for; matrix products, arithmetic and copies ran while one was open for 6% of the time, Pallas kernels for 0%

commit v1 on v0

--- a/solution.py
+++ b/solution.py
@@ -90,7 +90,7 @@
     for sweep_index in range(ITERS):
         orthonormal_images = operate(subspace)
         local_gram = jnp.dot(orthonormal_images, orthonormal_images.T, precision=FULL_PRECISION)
-        gram_matrix = lax.psum(local_gram, ("blk", "scale")) / node_total
+        gram_matrix = jnp.sum(lax.all_gather(local_gram, ("blk", "scale")), axis=0) / node_total
         factor = jnp.linalg.cholesky(gram_matrix)
         factor_inverse = jax.scipy.linalg.solve_triangular(
             factor, jnp.eye(vector_count, dtype=jnp.float32), lower=True

time: 409 us -> 672 us (1.64)
  waiting for transfers between devices: 3.48 us -> 433 us
  blocking collectives: 303 us -> 101 us
  other arithmetic: 26.5 us -> 43.4 us
  between operations: 1.87 us -> 15.2 us
  matrix products: 20.7 us -> 28.4 us
    all_gather x0 -> x2, waiting for transfers between devices: none -> 430 us  [shards(): lax.all_gather(local_gram, ('blk', 'scale'))]
    psum x2 -> x0, blocking collectives: 204 us -> none  [shards(): gram_matrix = lax.psum(local_gram, ('blk', 'scale')) / node_total]
    reduce_sum x0 -> x2, other arithmetic: none -> 13.9 us  [shards(): jnp.sum(lax.all_gather(local_gram, ('blk', 'scale')), axis=0) / node_total]
  transfers between devices with their start and end apart: 9 -> 11, of which waited for: 2 -> 4; matrix products, arithmetic and copies ran while one was open for 6% -> 5% of each run, Pallas kernels for 0% -> 0%
where the time goes in v1:
time: 672 us; the launch traced here: 671 us
  waiting for transfers between devices  433 us (64%)
  blocking collectives  101 us (15%)
  other arithmetic  43.4 us (6%)
  starting transfers between devices  38.3 us (6%)
  matrix products  28.4 us (4%)
  between operations  15.2 us (2%)
  local copies, waits for them, and re-layouts  11.6 us (2%)
    all_gather x2, waiting for transfers between devices, shards(): lax.all_gather(local_gram, ('blk', 'scale'))  430 us
    psum x1, blocking collectives, shards(): rayleigh = lax.psum(local_projection, ('blk', 'scale')) / node_total  101 us
    ppermute x6, starting transfers between devices, from_behind(): return lax.ppermute(block, axis, route)  25.1 us
    reduce_sum x2, other arithmetic, shards(): jnp.sum(lax.all_gather(local_gram, ('blk', 'scale')), axis=0) / node_total  13.9 us
  transfers between devices with their start and end apart: 11, of which 4 were waited for; matrix products, arithmetic and copies ran while one was open for 5% of the time, Pallas kernels for 0%

profile of v1, /device:TPU:1, one launch (start us, length us, event | category | flops | bytes accessed | tf_op | source)
XLA Modules:
  0.0 671.2 jit_solution(13167343540555966419)
XLA Ops:
  7.2 0.8 convert_rsqrt_fusion
  8.0 1.0 multiply_convert_fusion.2
  9.0 8.7 %collective-permute-start.2 = (bf16[64,1024]{1,0:T(8,128)(2,1)S(1)}, bf16[64,1024]{1,0:T(8,128)(2,1)S(1)}, u32[]{:S(2)}, u32[]{:S(2)}) collective-permute-start(bf16[64,1024]{1,0:T(8,128)(2,1)S(1)} %multiply_convert_fusion.2), channel_id=1, source_target_pairs={{0,1},{1,0},{2,3},{3,2},{4,5},{5,4},{6,7},{7,6},{8,9},{9,8},{10,11... | collective-permute-start | bytes 393224 | tf_op jit(solution)/shard_map/ppermute | solution.py:17
  17.7 1.0 fusion.136
  18.8 8.0 %collective-permute-start = (bf16[64,8,128]{2,1,0:T(8,128)(2,1)S(1)}, bf16[64,8,128]{2,1,0:T(8,128)(2,1)S(1)}, u32[]{:S(2)}, u32[]{:S(2)}) collective-permute-start(bf16[64,8,128]{2,1,0:T(8,128)(2,1)S(1)} %bitcast.145), channel_id=1, source_target_pairs={{8,0},{16,8},{24,16},{32,24},{40,32},{48,40},{56,48},{64,56},{72,6... | collective-permute-start | bytes 393224 | tf_op jit(solution)/shard_map/ppermute | solution.py:13
  28.1 1.0 fusion.83
  29.1 0.8 fusion.18
  29.9 1.2 fusion.3
  31.1 1.9 collective-permute-start.1
  33.1 1.2 fusion.16
  35.0 1.2 compare_and_fusion
  36.3 1.0 fusion.33
  37.8 3.2 gather_fusion
  41.2 2.0 convert_add_fusion.2
  43.2 2.1 fusion.118
  45.3 216.6 %all-gather.5.cloned.1.call-done = f32[32768,64]{1,0:T(8,128)} async-done(((f32[64,64]{1,0:T(8,128)}), f32[32768,64]{1,0:T(8,128)}) %all-gather.5.cloned.1.call-update) | async-done | bytes 8388624 | tf_op jit(solution)/shard_map/all_gather | solution.py:93
  261.9 6.9 %reduce_sum.18 = f32[64,64]{1,0:T(8,128)S(1)} reduce(f32[512,64,64]{2,1,0:T(8,128)} %bitcast.139, f32[]{:T(128)} %constant.49.clone.1), dimensions={0}, to_apply=%region_0.0 | reduce | flops 2093056 | bytes 8404996 | tf_op jit(solution)/shard_map/reduce_sum | solution.py:93
  269.1 5.8 cholesky.44
  276.3 4.9 custom-call.6
  281.8 2.2 collective-permute-start.5
  284.1 5.7 collective-permute-start.3
  290.1 0.8 fusion.20
  290.9 1.3 fusion.4
  292.2 1.9 collective-permute-start.4
  294.1 1.2 fusion.13
  295.3 1.0 fusion.37
  296.9 3.2 gather_fusion.1
  300.3 1.6 collective-permute-done.4
  301.9 1.9 convert_add_fusion.1
  303.8 1.8 fusion.122
  305.6 213.5 %all-gather.7.cloned.1.call-done = f32[32768,64]{1,0:T(8,128)} async-done(((f32[64,64]{1,0:T(8,128)}), f32[32768,64]{1,0:T(8,128)}) %all-gather.7.cloned.1.call-update) | async-done | bytes 8388624 | tf_op jit(solution)/shard_map/all_gather | solution.py:93
  519.1 6.9 %reduce_sum.19 = f32[64,64]{1,0:T(8,128)S(1)} reduce(f32[512,64,64]{2,1,0:T(8,128)} %bitcast.140, f32[]{:T(128)} %constant.49.clone.1), dimensions={0}, to_apply=%region_3.7 | reduce | flops 2093056 | bytes 8404996 | tf_op jit(solution)/shard_map/reduce_sum | solution.py:93
  526.3 5.8 cholesky.55
  533.4 4.9 custom-call.7
  538.6 1.0 multiply_convert_fusion
  539.6 2.2 collective-permute-start.8
  541.9 5.5 collective-permute-start.6
  547.3 1.0 fusion.79
  548.4 0.8 fusion.22
  549.2 1.2 fusion.5
  550.4 2.1 collective-permute-start.7
  552.6 1.2 fusion.10
  553.8 1.0 fusion.41
  555.4 3.2 gather_fusion.2
  558.8 1.4 collective-permute-done.7
  560.2 1.9 convert_add_fusion
  562.5 101.1 %psum.7 = f32[64,64]{0,1:T(8,128)S(1)} all-reduce(f32[64,64]{0,1:T(8,128)S(1)} %fusion.24), channel_id=1, replica_groups=mesh['blk'=64,'scale'=8] {'blk','scale'}, use_global_device_ids=true, to_apply=%region_4.8 | all-reduce | flops 4096 | bytes 32768 | tf_op jit(solution)/shard_map/psum | solution.py:101
  663.6 0.7 copy.42
  (62 shorter events, 8.3 us)
Async XLA Ops:
  7.2 21.9 %copy-start = (bf16[32,128,128]{2,1,0:T(8,128)(2,1)S(1)}, bf16[32,128,128]{2,1,0:T(8,128)(2,1)}, u32[]{:S(2)}) copy-start(bf16[32,128,128]{2,1,0:T(8,128)(2,1)} %param.13) | copy-start | bytes 3145732
  7.2 274.2 %copy-start.1 = (f32[64,1024]{1,0:T(8,128)S(1)}, f32[64,1024]{1,0:T(8,128)}, u32[]{:S(2)}) copy-start(f32[64,1024]{1,0:T(8,128)} %param.12) | copy-start | bytes 786436
  7.2 254.8 %all-gather.5.cloned.1.call-start = ((), (), s32[]{:S(2)}) async-start(), calls=%async_computation | async-start | bytes 16809984 | tf_op jit(solution)/shard_map/all_gather | solution.py:93
  9.0 28.6 %collective-permute-start.2 = (bf16[64,1024]{1,0:T(8,128)(2,1)S(1)}, bf16[64,1024]{1,0:T(8,128)(2,1)S(1)}, u32[]{:S(2)}, u32[]{:S(2)}) collective-permute-start(bf16[64,1024]{1,0:T(8,128)(2,1)S(1)} %multiply_convert_fusion.2), channel_id=1, source_target_pairs={{0,1},{1,0},{2,3},{3,2},{4,5},{5,4},{6,7},{7,6},{8,9},{9,8},{10,11... | collective-permute-start | bytes 393224 | tf_op jit(solution)/shard_map/ppermute | solution.py:17
  18.8 17.5 %collective-permute-start = (bf16[64,8,128]{2,1,0:T(8,128)(2,1)S(1)}, bf16[64,8,128]{2,1,0:T(8,128)(2,1)S(1)}, u32[]{:S(2)}, u32[]{:S(2)}) collective-permute-start(bf16[64,8,128]{2,1,0:T(8,128)(2,1)S(1)} %bitcast.145), channel_id=1, source_target_pairs={{8,0},{16,8},{24,16},{32,24},{40,32},{48,40},{56,48},{64,56},{72,6... | collective-permute-start | bytes 393224 | tf_op jit(solution)/shard_map/ppermute | solution.py:13
  27.4 8.9 %copy-start.3 = (f32[32]{0:T(128)}, f32[32]{0:T(128)S(1)}, u32[]{:S(2)}) copy-start(f32[32]{0:T(128)S(1)} %compare_convert_fusion) | copy-start | bytes 388
  31.1 10.0 %collective-permute-start.1 = (bf16[64,8,128]{2,1,0:T(8,128)(2,1)S(1)}, bf16[64,8,128]{2,1,0:T(8,128)(2,1)S(1)}, u32[]{:S(2)}, u32[]{:S(2)}) collective-permute-start(bf16[64,8,128]{2,1,0:T(8,128)(2,1)S(1)} %fusion.3), channel_id=1, source_target_pairs={{504,0},{0,8},{8,16},{16,24},{24,32},{32,40},{40,48},{48,56},{56,6... | collective-permute-start | bytes 393224 | tf_op jit(solution)/shard_map/ppermute | solution.py:13
  41.2 240.3 %copy-start.5 = (pred[1024]{0:T(1024)(128)(4,1)S(1)}, pred[1024]{0:T(1024)(128)(4,1)}, u32[]{:S(2)}) copy-start(pred[1024]{0:T(1024)(128)(4,1)} %compare_and_fusion) | copy-start | bytes 3076
  41.2 248.6 %copy-start.4 = (f32[32]{0:T(128)S(1)}, f32[32]{0:T(128)}, u32[]{:S(2)}) copy-start(f32[32]{0:T(128)} %copy-done.3) | copy-start | bytes 388
  41.2 248.6 %copy-start.7 = (s32[32]{0:T(128)S(1)}, s32[32]{0:T(128)}, u32[]{:S(2)}) copy-start(s32[32]{0:T(128)} %param.14) | copy-start | bytes 388
  45.3 473.8 %all-gather.7.cloned.1.call-start = ((), (), s32[]{:S(2)}) async-start(), calls=%async_computation.1 | async-start | bytes 16809984 | tf_op jit(solution)/shard_map/all_gather | solution.py:93
  281.8 14.9 %collective-permute-start.5 = (bf16[64,1024]{1,0:T(8,128)(2,1)S(1)}, bf16[64,1024]{1,0:T(8,128)(2,1)S(1)}, u32[]{:S(2)}, u32[]{:S(2)}) collective-permute-start(bf16[64,1024]{1,0:T(8,128)(2,1)S(1)} %get-tuple-element.9), channel_id=1, source_target_pairs={{0,1},{1,0},{2,3},{3,2},{4,5},{5,4},{6,7},{7,6},{8,9},{9,8},{10,11... | collective-permute-start | bytes 393224 | tf_op jit(solution)/shard_map/ppermute | solution.py:17
  284.1 11.3 %collective-permute-start.3 = (bf16[64,8,128]{2,1,0:T(8,128)(2,1)S(1)}, bf16[64,8,128]{2,1,0:T(8,128)(2,1)S(1)}, u32[]{:S(2)}, u32[]{:S(2)}) collective-permute-start(bf16[64,8,128]{2,1,0:T(8,128)(2,1)S(1)} %bitcast.151), channel_id=1, source_target_pairs={{8,0},{16,8},{24,16},{32,24},{40,32},{48,40},{56,48},{64,56},{72,6... | collective-permute-start | bytes 393224 | tf_op jit(solution)/shard_map/ppermute | solution.py:13
  292.2 9.7 %collective-permute-start.4 = (bf16[64,8,128]{2,1,0:T(8,128)(2,1)S(1)}, bf16[64,8,128]{2,1,0:T(8,128)(2,1)S(1)}, u32[]{:S(2)}, u32[]{:S(2)}) collective-permute-start(bf16[64,8,128]{2,1,0:T(8,128)(2,1)S(1)} %fusion.4), channel_id=1, source_target_pairs={{504,0},{0,8},{8,16},{16,24},{24,32},{32,40},{40,48},{48,56},{56,6... | collective-permute-start | bytes 393224 | tf_op jit(solution)/shard_map/ppermute | solution.py:13
  301.9 260.2 %copy-start.6 = (pred[1024]{0:T(1024)(128)(4,1)S(1)}, pred[1024]{0:T(1024)(128)(4,1)}, u32[]{:S(2)}) copy-start(pred[1024]{0:T(1024)(128)(4,1)} %compare_and_fusion) | copy-start | bytes 3076
  539.6 124.7 %copy-start.2 = (f32[64,1024]{1,0:T(8,128)}, f32[64,1024]{1,0:T(8,128)S(1)}, u32[]{:S(2)}) copy-start(f32[64,1024]{1,0:T(8,128)S(1)} %get-tuple-element.12) | copy-start | bytes 786436
  539.6 15.6 %collective-permute-start.8 = (bf16[64,1024]{1,0:T(8,128)(2,1)S(1)}, bf16[64,1024]{1,0:T(8,128)(2,1)S(1)}, u32[]{:S(2)}, u32[]{:S(2)}) collective-permute-start(bf16[64,1024]{1,0:T(8,128)(2,1)S(1)} %get-tuple-element.11), channel_id=1, source_target_pairs={{0,1},{1,0},{2,3},{3,2},{4,5},{5,4},{6,7},{7,6},{8,9},{9,8},{10,11... | collective-permute-start | bytes 393224 | tf_op jit(solution)/shard_map/ppermute | solution.py:17
  541.9 12.0 %collective-permute-start.6 = (bf16[64,8,128]{2,1,0:T(8,128)(2,1)S(1)}, bf16[64,8,128]{2,1,0:T(8,128)(2,1)S(1)}, u32[]{:S(2)}, u32[]{:S(2)}) collective-permute-start(bf16[64,8,128]{2,1,0:T(8,128)(2,1)S(1)} %bitcast.148), channel_id=1, source_target_pairs={{8,0},{16,8},{24,16},{32,24},{40,32},{48,40},{56,48},{64,56},{72,6... | collective-permute-start | bytes 393224 | tf_op jit(solution)/shard_map/ppermute | solution.py:13
  550.4 9.7 %collective-permute-start.7 = (bf16[64,8,128]{2,1,0:T(8,128)(2,1)S(1)}, bf16[64,8,128]{2,1,0:T(8,128)(2,1)S(1)}, u32[]{:S(2)}, u32[]{:S(2)}) collective-permute-start(bf16[64,8,128]{2,1,0:T(8,128)(2,1)S(1)} %fusion.5), channel_id=1, source_target_pairs={{504,0},{0,8},{8,16},{16,24},{24,32},{32,40},{40,48},{48,56},{56,6... | collective-permute-start | bytes 393224 | tf_op jit(solution)/shard_map/ppermute | solution.py:13
Sparse Core Ops, SparseCore 0:
  45.4 216.4 all-gather.4
  305.7 213.3 all-gather.6
